TPU v7x, 512 devices: a whole 4x4x16 slice. The times are simulated.
512 devices in a mesh: seq: 32 (over z, core), heads: 4 (over x), dp: 4 (over y).
Axes of the slice: x: 4, y: 4, z: 16, core: 2. Of those that a mesh axis runs over, the one named last changes fastest.
Arguments:
- tokens: bfloat16 [4, 4096, 3072], P('dp', 'seq'), may hold values from -6 to 6
- proj_weights: bfloat16 [3, 3072, 4096], P(None, 'seq', ('heads', 'dp')), may hold values from -0.109375 to 0.109375
- norm_gain: float32 [4096], P(('heads', 'dp')), may hold values from 0.5 to 1.5
Outputs:
- attended: bfloat16 [4, 4096, 4096], P('dp', 'seq', 'heads')
All inputs are finite; a program needn't handle non-finite values.
Results may differ from a plain program's by a relative error of at most 0.0063.
Values may be sent and summed in bfloat16 or wider, within the bound.
No kernel may reach another device: no remote copies, remote signals or barrier semaphores. Data moves between devices by JAX's collectives and lax.ppermute only.
A program may use at most 64 MiB of HBM per device.

v0:
```python
import jax
import jax.numpy as jnp
from jax import lax
from jax.sharding import PartitionSpec as P

DH = 128


def prefix_2(part, axis, combine, identity):
    place = lax.axis_index(axis)
    gathered = lax.all_gather(part, axis)
    state = jnp.zeros_like(part) + jnp.asarray(identity, part.dtype)

    def one(step, state):
        return combine(state, lax.dynamic_index_in_dim(gathered, step, 0, False))

    return lax.fori_loop(0, place, one, state)


def add_pair(earlier, later):
    return earlier + later


def project_rows(flat_rows):

    def accumulate(total, piece, start):
        return jnp.einsum("nd,jdc->jnc", flat_rows, piece, preferred_element_type=jnp.float32)

    return accumulate


def to_heads(matrix, seq_count, length):
    return matrix.reshape(seq_count, length, -1, DH)


def activate(matrix, seq_count, length):
    return to_heads(jax.nn.silu(matrix).astype(jnp.bfloat16), seq_count, length)


def block_prefix(keys_b, values_b):
    state = jnp.einsum("sthd,sthe->shde", keys_b, values_b, preferred_element_type=jnp.float32)
    return prefix_2(state, "seq", add_pair, jnp.zeros_like(state))


def attend(queries, keys_b, values_b, prefix, norm_gain):
    seq_count, length, head_count, head_size = queries.shape
    scores = jnp.einsum("sthd,suhd->shtu", queries, keys_b, preferred_element_type=jnp.float32)
    causal = lax.broadcasted_iota(jnp.int32, (length, length), 0) >= lax.broadcasted_iota(
        jnp.int32, (length, length), 1
    )
    scores_b = jnp.where(causal, scores, 0.0).astype(jnp.bfloat16)
    local = jnp.einsum("shtu,suhd->sthd", scores_b, values_b, preferred_element_type=jnp.float32)
    carried = jnp.einsum(
        "sthd,shde->sthe", queries, prefix.astype(jnp.bfloat16), preferred_element_type=jnp.float32
    )
    attn = local + carried
    scale = lax.rsqrt(jnp.mean(attn * attn, axis=-1, keepdims=True) + 1e-06)
    normed = attn * scale * norm_gain.reshape(head_count, head_size)
    return normed.astype(jnp.bfloat16).reshape(seq_count, length, head_count * head_size)


def body(tokens, proj_weights, norm_gain):
    everyone = lax.all_gather(tokens, "dp", axis=0, tiled=True)
    seq_count, length, width = everyone.shape
    total_rows = seq_count * length
    per_device = proj_weights.shape[2]
    accumulate = project_rows(everyone.reshape(total_rows, width))
    start_sum = jnp.zeros((3, total_rows, per_device), jnp.float32)
    projected = accumulate(
        start_sum, lax.all_gather(proj_weights, "seq", axis=1, tiled=True), jnp.int32(0)
    )
    queries = activate(projected[0], seq_count, length)
    keys_b = activate(projected[1], seq_count, length)
    values_b = to_heads(projected[2].astype(jnp.bfloat16), seq_count, length)
    prefix = block_prefix(keys_b, values_b)
    normed = attend(queries, keys_b, values_b, prefix, norm_gain)
    return lax.all_to_all(normed, "dp", split_axis=0, concat_axis=2, tiled=True)


def solution(mesh):
    in_specs = (P("dp", "seq", None), P(None, "seq", ("heads", "dp")), P(("heads", "dp")))
    out_specs = P("dp", "seq", "heads")
    return jax.shard_map(body, mesh=mesh, in_specs=in_specs, out_specs=out_specs, check_vma=False)
```

profile of v0, /device:TPU:481, one launch (start us, length us, event | category | flops | bytes accessed | tf_op | source)
XLA Modules:
  0.0 297.7 jit_solution(694654217346947341)
XLA Ops:
  8.1 47.7 %all-gather.7.cloned.1.call-done = bf16[4,128,3072]{2,1,0:T(8,128)(2,1)} async-done(((bf16[1,128,3072]{2,1,0:T(8,128)(2,1)}), bf16[4,128,3072]{2,1,0:T(8,128)(2,1)}) %all-gather.7.cloned.1.call-update) | async-done | bytes 3145744 | tf_op jit(solution)/shard_map/all_gather | solution.py:63
  55.8 76.4 %all-gather.5.cloned.1.call-done = bf16[3,3072,256]{2,1,0:T(8,128)(2,1)} async-done(((bf16[3,96,256]{2,1,0:T(8,128)(2,1)}), bf16[3,3072,256]{2,1,0:T(8,128)(2,1)}) %all-gather.5.cloned.1.call-update) | async-done | bytes 4718608 | tf_op jit(solution)/shard_map/all_gather | solution.py:70
  132.1 5.5 %convolution_bitcast_fusion = f32[3,512,256]{1,2,0:T(8,128)S(1)} fusion(bf16[3,3072,256]{2,1,0:T(8,128)(2,1)} %all-gather.5.cloned.1.call-done, bf16[512,3072,1]{1,0,2:T(8,128)(2,1)} %bitcast.33), kind=kOutput, calls=%fused_computation.1 | convolution fusion | flops 2415919104 | bytes 9437184 | tf_op jit(solution)/shard_map/nd,jdc->jnc/dot_general | solution.py:27
  140.6 101.5 %all-gather.9.cloned.1.call-done = f32[128,2,128,128]{3,2,1,0:T(8,128)} async-done(((f32[4,2,128,128]{3,2,1,0:T(8,128)}), f32[128,2,128,128]{3,2,1,0:T(8,128)}) %all-gather.9.cloned.1.call-update) | async-done | bytes 16777232 | tf_op jit(solution)/shard_map/all_gather | solution.py:11
  242.2 37.0 %while.10 = (s32[]{:T(128)}, f32[4,2,128,128]{3,2,1,0:T(8,128)S(1)}, s32[]{:T(128)}, f32[32,4,2,128,128]{4,3,2,1,0:T(8,128)}, s32[]{:T(128)}, /*index=5*/s32[]{:T(128)}, s32[]{:T(128)}) while((s32[]{:T(128)}, f32[4,2,128,128]{3,2,1,0:T(8,128)S(1)}, s32[]{:T(128)}, f32[32,4,2,128,128]{4,3,2,1,0:T(8,128)}, s32[]{:T(128)}, /*index=5*/s32[]{:T(128)}, ...), condition=%wide.region_1.2_spmd, body=%wide.region_0.1_spmd.sunk | while | flops 131077 | bytes 1572987 | solution.py:17
  242.2 1.2 bitcast_add_fusion.2
  243.4 1.2 bitcast_add_fusion.2
  244.6 1.2 bitcast_add_fusion.2
  245.8 1.2 bitcast_add_fusion.2
  247.0 1.2 bitcast_add_fusion.2
  251.7 1.2 bitcast_add_fusion.2
  252.9 1.2 bitcast_add_fusion.2
  254.1 1.2 bitcast_add_fusion.2
  255.3 1.2 bitcast_add_fusion.2
  256.5 1.2 bitcast_add_fusion.2
  257.7 1.2 bitcast_add_fusion.2
  263.7 1.2 bitcast_add_fusion.2
  264.9 1.2 bitcast_add_fusion.2
  266.0 1.2 bitcast_add_fusion.2
  267.2 1.2 bitcast_add_fusion.2
  268.4 1.2 bitcast_add_fusion.2
  269.6 1.2 bitcast_add_fusion.2
  274.4 1.2 bitcast_add_fusion.2
  279.7 10.6 %all_to_all.18 = bf16[4,128,256]{1,2,0:T(8,128)(2,1)S(1)} all-to-all(bf16[4,128,256]{1,2,0:T(8,128)(2,1)S(1)} %bitcast.29), channel_id=1, replica_groups=mesh['seq'=32,'heads'=4,'dp'=4] {'dp'}, dimensions={0} | all-to-all | bytes 524288 | tf_op jit(solution)/shard_map/all_to_all | solution.py:77
  (37 shorter events, 21.0 us)
Async XLA Ops:
  6.5 49.2 %all-gather.7.cloned.1.call-start = ((), (), s32[]{:S(2)}) async-start(), calls=%async_computation.2 | async-start | bytes 3932160 | tf_op jit(solution)/shard_map/all_gather | solution.py:63
  7.3 124.9 %all-gather.5.cloned.1.call-start = ((), (), s32[]{:S(2)}) async-start(), calls=%async_computation.1 | async-start | bytes 4866048 | tf_op jit(solution)/shard_map/all_gather | solution.py:70
  8.0 234.1 %all-gather.9.cloned.1.call-start = ((), (), s32[]{:S(2)}) async-start(), calls=%async_computation.3 | async-start | bytes 17301504 | tf_op jit(solution)/shard_map/all_gather | solution.py:11
  242.1 37.4 %copy-start = (f32[256]{0:T(256)S(1)}, f32[256]{0:T(256)}, u32[]{:S(2)}) copy-start(f32[256]{0:T(256)} %param.7) | copy-start | bytes 3076
Sparse Core Ops, SparseCore 0:
  9.5 46.2 all-gather.6
  57.9 74.1 all-gather.4
  139.7 102.3 all-gather.8
where the time goes:
time: 299 us; the launch traced here: 298 us
  waiting for transfers between devices  227 us (76%)
  other arithmetic  36.4 us (12%)
  between operations  13.2 us (4%)
  blocking collectives  10.6 us (4%)
  matrix products  7.57 us (3%)
    all_gather x1, waiting for transfers between devices, prefix_2(): gathered = lax.all_gather(part, axis)  101 us
    all_gather x1, waiting for transfers between devices, body(): lax.all_gather(proj_weights, 'seq', axis=1, tiled=True)  76.4 us
    all_gather x1, waiting for transfers between devices, body(): everyone = lax.all_gather(tokens, 'dp', axis=0, tiled=True)  47.7 us
    add x31, other arithmetic, add_pair(): return earlier + later  36.3 us
    all_to_all x1, blocking collectives, body(): return lax.all_to_all(normed, 'dp', split_axis=0, concat_axis=2, tiled=True)  10.6 us
  transfers between devices with their start and end apart: 3, of which 3 were waited for; matrix products, arithmetic and copies ran while one was open for 0% of the time, Pallas kernels for 0%

commit v1 on v0

--- a/solution.py
+++ b/solution.py
@@ -60,7 +60,12 @@
 
 
 def body(tokens, proj_weights, norm_gain):
-    everyone = lax.all_gather(tokens, "dp", axis=0, tiled=True)
+    ring = [tokens]
+    for hop in range(3):
+        ring.append(lax.ppermute(ring[-1], "dp", [(dev, (dev + 1) % 4) for dev in range(4)]))
+    everyone = jnp.roll(
+        jnp.concatenate(ring[::-1], axis=0), (lax.axis_index("dp") + 1) * ring[0].shape[0], axis=0
+    )
     seq_count, length, width = everyone.shape
     total_rows = seq_count * length
     per_device = proj_weights.shape[2]

time: 299 us -> 249 us (0.83)
  waiting for transfers between devices: 227 us -> 169 us
  starting transfers between devices: 0.08 us -> 7.1 us
    all_gather x1, waiting for transfers between devices: 76.4 us -> 10.9 us  [body(): lax.all_gather(proj_weights, 'seq', axis=1, tiled=True)]
    ppermute x0 -> x3, waiting for transfers between devices: none -> 55.3 us  [body(): lax.ppermute(ring[-1], 'dp', [(dev, (dev + 1) % 4) for dev in range(4)])]
    all_gather x1 -> x0, waiting for transfers between devices: 47.7 us -> none  [body(): everyone = lax.all_gather(tokens, 'dp', axis=0, tiled=True)]
    ppermute x0 -> x3, starting transfers between devices: none -> 7.06 us  [body(): lax.ppermute(ring[-1], 'dp', [(dev, (dev + 1) % 4) for dev in range(4)])]
  transfers between devices with their start and end apart: 3 -> 5, of which waited for: 3 -> 5; matrix products, arithmetic and copies ran while one was open for 0% -> 1% of each run, Pallas kernels for 0% -> 0%
where the time goes in v1:
time: 249 us; the launch traced here: 247 us
  waiting for transfers between devices  169 us (68%)
  other arithmetic  36.4 us (15%)
  between operations  13.6 us (5%)
  blocking collectives  10.6 us (4%)
  starting transfers between devices  7.1 us (3%)
  matrix products  6.99 us (3%)
  local copies, waits for them, and re-layouts  3.38 us (1%)
    all_gather x1, waiting for transfers between devices, prefix_2(): gathered = lax.all_gather(part, axis)  102 us
    ppermute x3, waiting for transfers between devices, body(): lax.ppermute(ring[-1], 'dp', [(dev, (dev + 1) % 4) for dev in range(4)])  55.3 us
    add x31, other arithmetic, add_pair(): return earlier + later  36.3 us
    all_gather x1, waiting for transfers between devices, body(): lax.all_gather(proj_weights, 'seq', axis=1, tiled=True)  10.9 us
    all_to_all x1, blocking collectives, body(): return lax.all_to_all(normed, 'dp', split_axis=0, concat_axis=2, tiled=True)  10.6 us
    ppermute x3, starting transfers between devices, body(): lax.ppermute(ring[-1], 'dp', [(dev, (dev + 1) % 4) for dev in range(4)])  7.06 us
  transfers between devices with their start and end apart: 5, of which 5 were waited for; matrix products, arithmetic and copies ran while one was open for 1% of the time, Pallas kernels for 0%

profile of v1, /device:TPU:481, one launch (start us, length us, event | category | flops | bytes accessed | tf_op | source)
XLA Modules:
  0.0 247.4 jit_solution(1460454438133815926)
XLA Ops:
  7.3 3.2 %collective-permute-start = (bf16[1,128,3072]{2,1,0:T(8,128)(2,1)}, bf16[1,128,3072]{2,1,0:T(8,128)(2,1)S(1)}, u32[]{:S(2)}, u32[]{:S(2)}) collective-permute-start(bf16[1,128,3072]{2,1,0:T(8,128)(2,1)} %param.5), channel_id=1, source_target_pairs={{0,1},{1,2},{2,3},{3,0},{4,5},{5,6},{6,7},{7,4},{8,9},{9,10},{10,1... | collective-permute-start | bytes 2359304 | tf_op jit(solution)/shard_map/ppermute | solution.py:65
  10.5 18.7 %collective-permute-done = bf16[1,128,3072]{2,1,0:T(8,128)(2,1)S(1)} collective-permute-done((bf16[1,128,3072]{2,1,0:T(8,128)(2,1)}, bf16[1,128,3072]{2,1,0:T(8,128)(2,1)S(1)}, u32[]{:S(2)}, u32[]{:S(2)}) %collective-permute-start) | collective-permute-done | bytes 786464 | tf_op jit(solution)/shard_map/ppermute | solution.py:65
  29.2 1.9 collective-permute-start.1
  31.1 18.7 %collective-permute-done.1 = bf16[1,128,3072]{2,1,0:T(8,128)(2,1)S(1)} collective-permute-done((bf16[1,128,3072]{2,1,0:T(8,128)(2,1)S(1)}, bf16[1,128,3072]{2,1,0:T(8,128)(2,1)S(1)}, u32[]{:S(2)}, u32[]{:S(2)}) %collective-permute-start.1) | collective-permute-done | bytes 786464 | tf_op jit(solution)/shard_map/ppermute | solution.py:65
  49.8 1.9 collective-permute-start.2
  51.8 17.9 %collective-permute-done.2 = bf16[1,128,3072]{2,1,0:T(8,128)(2,1)S(1)} collective-permute-done((bf16[1,128,3072]{2,1,0:T(8,128)(2,1)S(1)}, bf16[1,128,3072]{2,1,0:T(8,128)(2,1)S(1)}, u32[]{:S(2)}, u32[]{:S(2)}) %collective-permute-start.2) | collective-permute-done | bytes 786464 | tf_op jit(solution)/shard_map/ppermute | solution.py:65
  69.9 1.2 constant_dynamic-update-slice_fusion.4
  71.5 10.9 %all-gather.4.cloned.1.call-done = bf16[3,3072,256]{2,1,0:T(8,128)(2,1)} async-done(((bf16[3,96,256]{2,1,0:T(8,128)(2,1)}), bf16[3,3072,256]{2,1,0:T(8,128)(2,1)}) %all-gather.4.cloned.1.call-update) | async-done | bytes 4718608 | tf_op jit(solution)/shard_map/all_gather | solution.py:75
  82.4 4.9 %convolution_bitcast_fusion = f32[3,512,256]{2,1,0:T(8,128)S(1)} fusion(bf16[512,3072,1]{1,0,2:T(8,128)(2,1)S(1)} %bitcast.21, bf16[3,3072,256]{2,1,0:T(8,128)(2,1)} %all-gather.4.cloned.1.call-done), kind=kOutput, calls=%fused_computation.1 | convolution fusion | flops 2415919104 | bytes 9437184 | tf_op jit(solution)/shard_map/nd,jdc->jnc/dot_general | solution.py:27
  89.9 101.7 %all-gather.6.cloned.1.call-done = f32[128,2,128,128]{3,2,1,0:T(8,128)} async-done(((f32[4,2,128,128]{3,2,1,0:T(8,128)}), f32[128,2,128,128]{3,2,1,0:T(8,128)}) %all-gather.6.cloned.1.call-update) | async-done | bytes 16777232 | tf_op jit(solution)/shard_map/all_gather | solution.py:11
  191.6 37.0 %while.10 = (s32[]{:T(128)}, f32[4,2,128,128]{3,2,1,0:T(8,128)S(1)}, s32[]{:T(128)}, f32[32,4,2,128,128]{4,3,2,1,0:T(8,128)}, s32[]{:T(128)}, /*index=5*/s32[]{:T(128)}, s32[]{:T(128)}) while((s32[]{:T(128)}, f32[4,2,128,128]{3,2,1,0:T(8,128)S(1)}, s32[]{:T(128)}, f32[32,4,2,128,128]{4,3,2,1,0:T(8,128)}, s32[]{:T(128)}, /*index=5*/s32[]{:T(128)}, ...), condition=%wide.region_1.2_spmd, body=%wide.region_0.1_spmd.sunk | while | flops 131077 | bytes 1572987 | solution.py:17
  191.6 1.2 bitcast_add_fusion.2
  192.8 1.2 bitcast_add_fusion.2
  194.0 1.2 bitcast_add_fusion.2
  195.2 1.2 bitcast_add_fusion.2
  196.4 1.2 bitcast_add_fusion.2
  197.6 1.2 bitcast_add_fusion.2
  202.4 1.2 bitcast_add_fusion.2
  203.6 1.2 bitcast_add_fusion.2
  204.8 1.2 bitcast_add_fusion.2
  206.0 1.2 bitcast_add_fusion.2
  207.2 1.2 bitcast_add_fusion.2
  208.3 1.2 bitcast_add_fusion.2
  229.1 10.6 %all_to_all.18 = bf16[4,128,256]{1,2,0:T(8,128)(2,1)S(1)} all-to-all(bf16[4,128,256]{1,2,0:T(8,128)(2,1)S(1)} %bitcast.22), channel_id=1, replica_groups=mesh['seq'=32,'heads'=4,'dp'=4] {'dp'}, dimensions={0} | all-to-all | bytes 524288 | tf_op jit(solution)/shard_map/all_to_all | solution.py:82
  (48 shorter events, 27.4 us)
Async XLA Ops:
  6.5 64.7 %copy-start = (bf16[1,128,3072]{2,1,0:T(8,128)(2,1)S(1)}, bf16[1,128,3072]{2,1,0:T(8,128)(2,1)}, u32[]{:S(2)}) copy-start(bf16[1,128,3072]{2,1,0:T(8,128)(2,1)} %param.5) | copy-start | bytes 2359300
  6.5 75.9 %all-gather.4.cloned.1.call-start = ((), (), s32[]{:S(2)}) async-start(), calls=%async_computation.1 | async-start | bytes 4866048 | tf_op jit(solution)/shard_map/all_gather | solution.py:75
  7.3 184.3 %all-gather.6.cloned.1.call-start = ((), (), s32[]{:S(2)}) async-start(), calls=%async_computation.2 | async-start | bytes 17301504 | tf_op jit(solution)/shard_map/all_gather | solution.py:11
  7.3 21.9 %collective-permute-start = (bf16[1,128,3072]{2,1,0:T(8,128)(2,1)}, bf16[1,128,3072]{2,1,0:T(8,128)(2,1)S(1)}, u32[]{:S(2)}, u32[]{:S(2)}) collective-permute-start(bf16[1,128,3072]{2,1,0:T(8,128)(2,1)} %param.5), channel_id=1, source_target_pairs={{0,1},{1,2},{2,3},{3,0},{4,5},{5,6},{6,7},{7,4},{8,9},{9,10},{10,1... | collective-permute-start | bytes 2359304 | tf_op jit(solution)/shard_map/ppermute | solution.py:65
  29.2 20.7 %collective-permute-start.1 = (bf16[1,128,3072]{2,1,0:T(8,128)(2,1)S(1)}, bf16[1,128,3072]{2,1,0:T(8,128)(2,1)S(1)}, u32[]{:S(2)}, u32[]{:S(2)}) collective-permute-start(bf16[1,128,3072]{2,1,0:T(8,128)(2,1)S(1)} %collective-permute-done), channel_id=1, source_target_pairs={{0,1},{1,2},{2,3},{3,0},{4,5},{5,6},{6,7},{7,4},{8,9},{9,10},{10,1... | collective-permute-start | bytes 2359304 | tf_op jit(solution)/shard_map/ppermute | solution.py:65
  49.8 19.8 %collective-permute-start.2 = (bf16[1,128,3072]{2,1,0:T(8,128)(2,1)S(1)}, bf16[1,128,3072]{2,1,0:T(8,128)(2,1)S(1)}, u32[]{:S(2)}, u32[]{:S(2)}) collective-permute-start(bf16[1,128,3072]{2,1,0:T(8,128)(2,1)S(1)} %collective-permute-done.1), channel_id=1, source_target_pairs={{0,1},{1,2},{2,3},{3,0},{4,5},{5,6},{6,7},{7,4},{8,9},{9,10},{10,1... | collective-permute-start | bytes 2359304 | tf_op jit(solution)/shard_map/ppermute | solution.py:65
  89.9 139.1 %copy-start.1 = (f32[256]{0:T(256)S(1)}, f32[256]{0:T(256)}, u32[]{:S(2)}) copy-start(f32[256]{0:T(256)} %param.7) | copy-start | bytes 3076
Sparse Core Ops, SparseCore 0:
  9.5 72.8 all-gather.3
  89.1 102.4 all-gather.5
